TPU v7x, 1024 devices: a whole 8x8x8 slice. The times are simulated.
1024 devices in a mesh: blk: 32 (over x, z_hi, core), trial: 4 (over z_lo), val: 8 (over y).
Axes of the slice: x: 8, y: 8, z: 8 (z_hi: 2, z_lo: 4; z = z_hi * 4 + z_lo), core: 2. Of those that a mesh axis runs over, the one named last changes fastest.
Arguments:
- trials: bfloat16 [32, 256, 512], P(None, None, 'trial'), may hold values from -6 to 6
- valence_factor: bfloat16 [512, 256, 256], P('blk', 'val'), may hold values from -0.015625 to 0.015625
- conduction_factor: bfloat16 [512, 512, 512], P('blk', 'trial'), may hold values from -0.25 to 0.25
- val_energy: float32 [256], P('val'), may hold values from -3 to -0.5
- cond_energy: float32 [512], P('trial'), may hold values from 0.5 to 3
Outputs:
- applied: float32 [32, 256, 512], P(None, 'val', 'trial')
- residual: float32 [32, 256, 512], P(None, 'val', 'trial')
- quotient: float32 [32], replicated
All inputs are finite; a program needn't handle non-finite values.
Results may differ from a plain program's by a relative error of at most 0.002.
Values sent between devices are 32-bit elements; how exact they have to be, the bound alone decides.
A program may use at most 32 MiB of HBM per device.

v0:
```python
import functools

import jax
import jax.numpy as jnp
from jax import lax
from jax.sharding import Mesh
from jax.sharding import PartitionSpec as P

BLK = ("blk_0", "blk_1", "blk_2")
BLK_TRIAL_VAL = ("blk_0", "blk_1", "blk_2", "trial", "val")


def split_up(shard, dim, peers):
    lengths = shard.shape
    pieces = shard.reshape(*lengths[:dim], peers, lengths[dim] // peers, *lengths[dim + 1 :])
    return jnp.moveaxis(pieces, dim, 0)


def sum_at_owner(shard, axis, dim):
    peers = lax.axis_size(axis)
    pieces = lax.all_to_all(split_up(shard, dim, peers), axis, 0, 0, tiled=True)
    return jnp.sum(pieces, axis=0)


def by_axis(shard, axes):
    return functools.reduce(lax.psum, axes, shard)


def side_by_side(arrays, axis, dim, along):
    ends, at = ([], 0)
    for a in arrays[:-1]:
        at += a.shape[along]
        ends.append(at)
    both = jnp.concatenate(arrays, axis=along)
    return tuple(jnp.split(lax.all_gather(both, axis, axis=dim, tiled=True), ends, axis=along))


def on_device(trials, valence_factor, conduction_factor, val_energy, cond_energy):
    trial_count = trials.shape[0]
    row_count = valence_factor.shape[1]
    col_count = cond_energy.shape[0]
    row_start = lax.axis_index("val") * row_count
    inner = jnp.einsum(
        "pvw,twc->ptvc", valence_factor, trials, preferred_element_type=jnp.float32
    ).astype(jnp.bfloat16)
    partial_sum = jnp.einsum(
        "ptvc,pcd->tvd", inner, conduction_factor, preferred_element_type=jnp.float32
    )
    trial_block = lax.dynamic_slice_in_dim(trials, row_start, row_count, 1).astype(jnp.float32)
    energy = cond_energy[None, :] - val_energy[:, None]
    columns = sum_at_owner(partial_sum, "trial", 2)
    flat_rows = trial_count * row_count
    flat_direct = columns.reshape(flat_rows, col_count)
    share = sum_at_owner(flat_direct, BLK, 0)
    share_rows = share.shape[0]
    share_start = lax.axis_index(BLK) * share_rows
    trial_flat = trial_block.reshape(flat_rows, col_count)
    trial_share = lax.dynamic_slice_in_dim(trial_flat, share_start, share_rows, 0)
    energy_flat = jnp.tile(energy, (trial_count, 1))
    energy_share = lax.dynamic_slice_in_dim(energy_flat, share_start, share_rows, 0)
    applied_share = share + energy_share * trial_share
    owner = (share_start + jnp.arange(share_rows, dtype=jnp.int32)) // row_count
    selector = (owner[:, None] == jnp.arange(trial_count, dtype=jnp.int32)[None, :]).astype(
        jnp.float32
    )
    row_products = jnp.sum(trial_share * applied_share, axis=1)
    row_squares = jnp.sum(trial_share * trial_share, axis=1)
    numer_part = jnp.sum(selector * row_products[:, None], axis=0)
    denom_part = jnp.sum(selector * row_squares[:, None], axis=0)
    numerator, denom_sum = (by_axis(numer_part, BLK_TRIAL_VAL), by_axis(denom_part, BLK_TRIAL_VAL))
    quotient = numerator / (denom_sum + 1e-06)
    row_quotient = jnp.sum(selector * quotient[None, :], axis=1)
    residual_share = applied_share - row_quotient[:, None] * trial_share
    applied_flat, residual_flat = side_by_side((applied_share, residual_share), BLK, 0, 1)
    applied = applied_flat.reshape(trial_count, row_count, col_count)
    residual = residual_flat.reshape(trial_count, row_count, col_count)
    return (applied, residual, quotient)


def solution(mesh):
    split = Mesh(
        mesh.devices.reshape(8, 2, 2, mesh.shape["trial"], mesh.shape["val"]),
        ("blk_0", "blk_1", "blk_2", "trial", "val"),
    )
    in_specs = (
        P(None, None, "trial"),
        P(BLK, "val", None),
        P(BLK, "trial", None),
        P("val"),
        P("trial"),
    )
    out_specs = (P(None, "val", "trial"), P(None, "val", "trial"), P())
    return jax.shard_map(
        on_device, mesh=split, in_specs=in_specs, out_specs=out_specs, check_vma=False
    )
```

profile of v0, /device:TPU:1, one launch (start us, length us, event | category | flops | bytes accessed | tf_op | source)
XLA Modules:
  0.0 268.4 jit_solution(1814745446767450735)
XLA Ops:
  7.2 0.0 copy-start
  7.2 1.6 copy-done
  8.8 6.5 %fusion.8 = f32[32,4,4,8,128]{4,3,2,1,0:T(8,128)} fusion(bf16[16,128,512]{2,1,0:T(8,128)(2,1)} %param.7, bf16[32,256,128]{2,1,0:T(8,128)(2,1)S(1)} %copy-done, bf16[16,32,256]{2,1,0:T(8,128)(2,1)} %param.6), kind=kOutput, calls=%fused_computation.7 | convolution fusion | flops 3223322624 | bytes 6553600 | tf_op jit(solution)/shard_map/ptvc,pcd->tvd/dot_general | solution.py:46
  15.2 1.9 copy.14
  17.1 56.1 %all_to_all.10 = f32[4,32,32,128]{3,2,1,0:T(8,128)} all-to-all(f32[4,32,32,128]{3,2,1,0:T(8,128)S(1)} %bitcast.37), channel_id=1, replica_groups=mesh['blk_0'=8,'blk_1'=2,'blk_2'=2,'trial'=4,'val'=8] {'trial'}, dimensions={0} | all-to-all | bytes 4194304 | tf_op jit(solution)/shard_map/all_to_all | solution.py:21
  73.2 0.0 copy-start.1
  73.2 0.0 copy-start.2
  73.2 2.7 reduce_sum.63
  75.8 19.8 %all-to-all-start.1 = ((f32[32,32,128]{2,1,0:T(8,128)}), f32[32,32,128]{2,1,0:T(8,128)S(1)}, u32[]{:S(2)}, u32[]{:S(2)}) async-start(f32[32,32,128]{2,1,0:T(8,128)} %reduce_sum.63), calls=%async_computation.1 | async-start | bytes 1048576 | tf_op jit(solution)/shard_map/all_to_all | solution.py:21
  95.7 0.0 all-gather.2.cloned.1.call-start
  95.8 0.0 copy-done.1
  95.8 0.0 copy-done.2
  95.8 0.1 broadcast_subtract_fusion
  95.9 18.2 %all-to-all-done.1 = f32[32,32,128]{2,1,0:T(8,128)S(1)} async-done(((f32[32,32,128]{2,1,0:T(8,128)}), f32[32,32,128]{2,1,0:T(8,128)S(1)}, u32[]{:S(2)}, u32[]{:S(2)}) %all-to-all-start.1) | async-done | bytes 524320 | tf_op jit(solution)/shard_map/all_to_all | solution.py:21
  114.1 0.1 tile.4
  114.2 0.1 fusion.20
  114.3 0.1 select_reduce_fusion.1
  114.4 12.6 %all-reduce.1 = (f32[32]{0:T(128)S(1)}, f32[32]{0:T(128)S(1)}) all-reduce(f32[32]{0:T(128)S(1)} %get-tuple-element.6, f32[32]{0:T(128)S(1)} %get-tuple-element.5), channel_id=1, replica_groups=mesh['blk_0'=8,'blk_1'=2,'blk_2'=2,'trial'=4,'val'=8] {'blk_0'}, use_global_device_ids=true, to_apply=%region_4.5 | all-reduce | flops 64 | bytes 512 | tf_op jit(solution)/shard_map/psum | solution.py:26
  126.9 7.7 %all-reduce.4 = (f32[32]{0:T(128)S(1)}, f32[32]{0:T(128)S(1)}) all-reduce(f32[32]{0:T(128)S(1)} %get-tuple-element.9, f32[32]{0:T(128)S(1)} %get-tuple-element.10), channel_id=1, replica_groups=mesh['blk_0'=8,'blk_1'=2,'blk_2'=2,'trial'=4,'val'=8] {'blk_1'}, use_global_device_ids=true, to_apply=%region_5.6 | all-reduce | flops 64 | bytes 512 | tf_op jit(solution)/shard_map/psum | solution.py:26
  134.6 8.5 %all-reduce.3 = (f32[32]{0:T(128)S(1)}, f32[32]{0:T(128)S(1)}) all-reduce(f32[32]{0:T(128)S(1)} %get-tuple-element.15, f32[32]{0:T(128)S(1)} %get-tuple-element.16), channel_id=1, replica_groups=mesh['blk_0'=8,'blk_1'=2,'blk_2'=2,'trial'=4,'val'=8] {'blk_2'}, use_global_device_ids=true, to_apply=%region_6.7 | all-reduce | flops 64 | bytes 512 | tf_op jit(solution)/shard_map/psum | solution.py:26
  143.1 7.9 %all-reduce.2 = (f32[32]{0:T(128)S(1)}, f32[32]{0:T(128)S(1)}) all-reduce(f32[32]{0:T(128)S(1)} %get-tuple-element.13, f32[32]{0:T(128)S(1)} %get-tuple-element.14), channel_id=1, replica_groups=mesh['blk_0'=8,'blk_1'=2,'blk_2'=2,'trial'=4,'val'=8] {'trial'}, use_global_device_ids=true, to_apply=%region_7.8 | all-reduce | flops 64 | bytes 512 | tf_op jit(solution)/shard_map/psum | solution.py:26
  151.0 14.6 %all-reduce = (f32[32]{0:T(128)S(1)}, f32[32]{0:T(128)S(1)}) all-reduce(f32[32]{0:T(128)S(1)} %get-tuple-element.11, f32[32]{0:T(128)S(1)} %get-tuple-element.12), channel_id=1, replica_groups=mesh['blk_0'=8,'blk_1'=2,'blk_2'=2,'trial'=4,'val'=8] {'val'}, use_global_device_ids=true, to_apply=%region_8.9 | all-reduce | flops 64 | bytes 512 | tf_op jit(solution)/shard_map/psum | solution.py:26
  165.6 0.0 copy-start.3
  165.7 0.2 select_reduce_fusion
  165.8 0.1 fusion.17
  165.9 0.6 pad_maximum_fusion
  166.5 0.0 all-gather.2.cloned.1.call-update
  166.6 92.7 %all-gather.2.cloned.1.call-done = f32[1024,256]{1,0:T(8,128)} async-done(((f32[32,256]{1,0:T(8,128)}), f32[1024,256]{1,0:T(8,128)}) %all-gather.2.cloned.1.call-update) | async-done | bytes 1048592 | tf_op jit(solution)/shard_map/all_gather | solution.py:35
  259.3 2.2 fusion.22
  261.5 0.0 copy-done.3
  (4 shorter events, 0.1 us)
Async XLA Ops:
  7.2 1.6 copy-start
  73.2 22.6 %copy-start.1 = (f32[32]{0:T(128)S(1)}, f32[32]{0:T(128)}, u32[]{:S(2)}) copy-start(f32[32]{0:T(128)} %param.8) | copy-start | bytes 388
  73.2 22.6 %copy-start.2 = (f32[128]{0:T(128)S(1)}, f32[128]{0:T(128)}, u32[]{:S(2)}) copy-start(f32[128]{0:T(128)} %param.9) | copy-start | bytes 1540
  75.8 38.2 %all-to-all-start.1 = ((f32[32,32,128]{2,1,0:T(8,128)}), f32[32,32,128]{2,1,0:T(8,128)S(1)}, u32[]{:S(2)}, u32[]{:S(2)}) async-start(f32[32,32,128]{2,1,0:T(8,128)} %reduce_sum.63), calls=%async_computation.1 | async-start | bytes 1048576 | tf_op jit(solution)/shard_map/all_to_all | solution.py:21
  95.7 163.6 %all-gather.2.cloned.1.call-start = ((), (), s32[]{:S(2)}) async-start(), calls=%async_computation.2 | async-start | bytes 1081344 | tf_op jit(solution)/shard_map/all_gather | solution.py:35
  165.6 95.9 %copy-start.3 = (f32[32]{0:T(128)}, f32[32]{0:T(128)S(1)}, u32[]{:S(2)}) copy-start(f32[32]{0:T(128)S(1)} %add_divide_fusion) | copy-start | bytes 388
Sparse Core Ops, SparseCore 0:
  166.7 92.5 all-gather.1
where the time goes:
time: 269 us; the launch traced here: 268 us
  waiting for transfers between devices  111 us (41%)
  blocking collectives  107 us (40%)
  starting transfers between devices  19.9 us (7%)
  between operations  14.1 us (5%)
  matrix products  6.46 us (2%)
  local copies, waits for them, and re-layouts  5.78 us (2%)
  other arithmetic  3.9 us (1%)
    all_gather x1, waiting for transfers between devices, side_by_side(): lax.all_gather(both, axis, axis=dim, tiled=True)  92.7 us
    all_to_all x1, blocking collectives, sum_at_owner(): pieces = lax.all_to_all(split_up(shard, dim, peers), axis, 0, 0, tiled=True)  56.1 us
    psum x5, blocking collectives, by_axis(): return functools.reduce(lax.psum, axes, shard)  51.3 us
    all_to_all x1, starting transfers between devices, sum_at_owner(): pieces = lax.all_to_all(split_up(shard, dim, peers), axis, 0, 0, tiled=True)  19.8 us
    all_to_all x1, waiting for transfers between devices, sum_at_owner(): pieces = lax.all_to_all(split_up(shard, dim, peers), axis, 0, 0, tiled=True)  18.2 us
    dot_general x1, matrix products, on_device(): jnp.einsum('ptvc,pcd->tvd', inner, conduction_factor, preferred_element_t...  6.46 us
  transfers between devices with their start and end apart: 2, of which 2 were waited for; matrix products, arithmetic and copies ran while one was open for 0% of the time, Pallas kernels for 0%

commit v1 on v0

v1 whole, which is shorter than its diff:
```python
import functools

import jax
import jax.numpy as jnp
from jax import lax
from jax.experimental import pallas as pl
from jax.experimental.pallas import tpu as pltpu
from jax.sharding import Mesh
from jax.sharding import PartitionSpec as P

BLK = ("x", "zh", "core")
MESH = pl.DeviceIdType.MESH
RING = 8
PAIR_ROWS = 64
SUBS = 4
SUB_ROWS = PAIR_ROWS // SUBS
TARGET = (4, 3, 5, 2, 6, 1, 7, 0)
SLOT_UP = (0, 1, 3, 5, 7)
SLOT_DOWN = (0, 2, 4, 6, 7)


def ring(i):
    return lax.rem(i, RING)


def kernel(
    trials_hbm, valence_hbm, conduction_hbm, energy_ref,
    applied_ref, residual_ref, quotient_ref,
    trials, valence, conduction, left, outgoing, from_core, own, from_x, blocks, from_z,
    gathered, sums, sums_z, sums_y, quotients,
    load_sem, core_send, core_recv, x_send, x_recv, z_send, z_recv, g_send, g_recv,
    f_send, f_recv, qz_send, qz_recv, qy_send, qy_recv, qx_send, qx_recv,
):
    x, zh, core = lax.axis_index("x"), lax.axis_index("zh"), lax.axis_index("core")
    zl, y = lax.axis_index("trial"), lax.axis_index("val")
    z = zh * 4 + zl
    other = 1 - core

    def at_x(step, c):
        return {"x": ring(x + step), "zh": zh, "core": c, "trial": zl, "val": y}

    def at_z(step):
        there = ring(z + step)
        return {"x": x, "zh": there // 4, "core": core, "trial": lax.rem(there, 4), "val": y}

    def at_y(step):
        return {"x": x, "zh": zh, "core": core, "trial": zl, "val": ring(y + step)}

    def remote(src, dst, send, recv, device):
        return pltpu.make_async_remote_copy(
            src_ref=src, dst_ref=dst, send_sem=send, recv_sem=recv,
            device_id=device, device_id_type=MESH,
        )

    loads = [
        pltpu.make_async_copy(valence_hbm, valence, load_sem.at[0]),
        pltpu.make_async_copy(trials_hbm, trials, load_sem.at[1]),
        pltpu.make_async_copy(conduction_hbm, conduction, load_sem.at[2]),
    ]
    for load in loads:
        load.start()
    barrier = pltpu.get_barrier_semaphore()
    partners = [at_x(0, other)]
    for step in range(1, RING):
        partners += [at_x(step, core), at_x(step, other), at_z(step), at_y(step)]
    for device in partners:
        pl.semaphore_signal(barrier, inc=1, device_id=device, device_id_type=MESH)
    loads[0].wait()
    loads[1].wait()

    def unit(half, u):
        for q in range(4):
            first = 16 * half + 2 * ring(x + TARGET[4 * u + q])
            pair = jnp.concatenate([trials[first], trials[first + 1]], axis=1)
            inner = jnp.dot(valence[...], pair, preferred_element_type=jnp.float32)
            inner = inner.astype(jnp.bfloat16)
            for p in range(16):
                for i in range(2):
                    left[q * 64 + i * 32:q * 64 + i * 32 + 32, p * 128:(p + 1) * 128] = (
                        inner[p * 32:(p + 1) * 32, i * 128:(i + 1) * 128]
                    )
        if half is other and u == 0:
            loads[2].wait()
        return jnp.dot(left[...], conduction[...], preferred_element_type=jnp.float32)

    to_core = []
    for u in range(2):
        outgoing[u] = unit(other, u)
        if u == 0:
            pl.semaphore_wait(barrier, len(partners))
        copy = remote(outgoing.at[u], from_core.at[u], core_send.at[u], core_recv.at[u],
                      at_x(0, other))
        copy.start()
        to_core.append(copy)

    x_copies = {}

    def send_x(way, hop, s):
        slot = (SLOT_UP, SLOT_DOWN)[way][hop]
        rows = pl.ds(s * SUB_ROWS, SUB_ROWS)
        copy = remote(own.at[slot, rows], from_x.at[way, hop, s], x_send.at[way, hop, s],
                      x_recv.at[way, hop, s], at_x((1, 7)[way], core))
        copy.start()
        x_copies[way, hop, s] = copy

    def long_chain(way, s):
        return (s < SUBS // 2) == (way == 0)

    for u in range(2):
        product = unit(core, u)
        to_core[u].wait_recv()
        for q in range(4):
            own[4 * u + q] = product[q * 64:(q + 1) * 64] + from_core[u, q * 64:(q + 1) * 64]
        if u == 0:
            for s in range(SUBS):
                for way in range(2):
                    if long_chain(way, s):
                        send_x(way, 0, s)
            for s in range(SUBS):
                for way in range(2):
                    if not long_chain(way, s):
                        send_x(way, 1, s)
    for turn in range(4):
        for s in range(SUBS):
            for way in range(2):
                hop = turn if long_chain(way, s) else turn + 1
                if hop > 3:
                    continue
                x_copies[way, hop, s].wait_recv()
                slot = (SLOT_UP, SLOT_DOWN)[way][hop + 1]
                rows = slice(s * SUB_ROWS, (s + 1) * SUB_ROWS)
                own[slot, rows] = own[slot, rows] + from_x[way, hop, s]
                if hop < 3:
                    send_x(way, hop + 1, s)

    for b in range(4):
        blocks[b] = own[7, :, b * 128:(b + 1) * 128]
    z_copies = {}
    for step in (4, 3, 5, 2, 6, 1, 7):
        block = lax.rem(zl + step, 4)
        copy = remote(blocks.at[block], from_z.at[step], z_send.at[step], z_recv.at[step], at_z(step))
        copy.start()
        z_copies[step] = copy
    from_z[0] = blocks[zl]
    for step in (1, 7, 2, 6, 3, 5, 4):
        z_copies[step].wait_recv()
    total = from_z[ring(z + RING)]
    for i in range(1, RING):
        total = total + from_z[ring(z + RING - i)]
    mine = core * 16 + x * 2
    v_rows = pl.ds(pl.multiple_of(y * 32, 32), 32)
    energy = energy_ref[...]
    products = []
    squares = []
    for i in range(2):
        vector = trials[mine + i, v_rows, :].astype(jnp.float32)
        image = total[i * 32:(i + 1) * 32] + energy * vector
        gathered[mine + i] = image
        products.append(jnp.sum(vector * image, axis=0, keepdims=True))
        squares.append(jnp.sum(vector * vector, axis=0, keepdims=True))
    sums_z[0] = jnp.concatenate(products + squares, axis=0)

    q_copies = []
    for step, slot in ((1, 3), (7, 1), (2, 2)):
        copy = remote(sums_z.at[0], sums_z.at[slot], qz_send.at[slot], qz_recv.at[slot], at_z(step))
        copy.start()
        q_copies.append(copy)
    g_copies = {}
    pair = pl.ds(mine, 2)
    for step in (4, 3, 5, 2, 6, 1, 7):
        copy = remote(gathered.at[pair], gathered.at[pair], g_send.at[step], g_recv.at[step],
                      at_x(step, core))
        copy.start()
        g_copies[step] = copy
    f_copies = {}

    def forward(step):
        there = pl.ds(core * 16 + 2 * ring(x + RING - step), 2)
        if step:
            g_copies[step].wait_recv()
        copy = remote(gathered.at[there], gathered.at[there], f_send.at[step], f_recv.at[step],
                      at_x(0, other))
        copy.start()
        f_copies[step] = copy

    forward(0)
    for copy in q_copies:
        copy.wait_recv()
    total = sums_z[lax.rem(4 - zl, 4)]
    for i in range(1, 4):
        total = total + sums_z[lax.rem(4 - zl + i, 4)]
    sums_y[0] = total
    y_copies = []
    for step in (4, 3, 5, 2, 6, 1, 7):
        copy = remote(sums_y.at[0], sums_y.at[step], qy_send.at[step], qy_recv.at[step], at_y(step))
        copy.start()
        y_copies.append(copy)
    for step in (1, 7, 2):
        forward(step)
    for copy in y_copies:
        copy.wait_recv()
    total = sums_y[ring(y + RING)]
    for i in range(1, RING):
        total = total + sums_y[ring(y + RING - i)]
    lanes = jnp.sum(total, axis=1, keepdims=True)
    ratio = lanes[0:2] / (lanes[2:4] + 1e-6)
    seat = core * 8 + x
    quotients[seat] = jnp.broadcast_to(ratio, (2, 128))
    for n in range(1, 16):
        step, c = n // 2, (core if n % 2 == 0 else other)
        copy = remote(quotients.at[seat], quotients.at[seat], qx_send.at[n], qx_recv.at[n], at_x(step, c))
        copy.start()
        q_copies.append(copy)
    for step in (6, 3, 5, 4):
        forward(step)
    for copy in q_copies[3:]:
        copy.wait_recv()
    for step in range(RING):
        f_copies[step].wait_recv()
    for n in range(16):
        for i in range(2):
            t = 2 * n + i
            row = quotients[n, i:i + 1, :]
            image = gathered[t]
            applied_ref[t] = image
            residual_ref[t] = image - row * trials[t, v_rows, :].astype(jnp.float32)
            quotient_ref[t:t + 1, :] = row
    for group in (to_core, x_copies.values(), z_copies.values(), g_copies.values(), f_copies.values(),
                  q_copies, y_copies):
        for copy in group:
            copy.wait_send()


def on_device(trials, valence_factor, conduction_factor, val_energy, cond_energy):
    energy = cond_energy[None, :] - val_energy[:, None]
    vmem = pl.BlockSpec(memory_space=pltpu.VMEM)
    hbm = pl.BlockSpec(memory_space=pl.ANY)
    dma = pltpu.SemaphoreType.DMA
    f32 = jnp.float32
    applied, residual, quotient = pl.pallas_call(
        kernel,
        out_shape=(
            jax.ShapeDtypeStruct((32, 32, 128), f32),
            jax.ShapeDtypeStruct((32, 32, 128), f32),
            jax.ShapeDtypeStruct((32, 128), f32),
        ),
        in_specs=[hbm, hbm, hbm, vmem],
        out_specs=(vmem, vmem, vmem),
        scratch_shapes=[
            pltpu.VMEM((32, 256, 128), jnp.bfloat16),
            pltpu.VMEM((512, 256), jnp.bfloat16),
            pltpu.VMEM((2048, 512), jnp.bfloat16),
            pltpu.VMEM((256, 2048), jnp.bfloat16),
            pltpu.VMEM((2, 256, 512), f32),
            pltpu.VMEM((2, 256, 512), f32),
            pltpu.VMEM((8, PAIR_ROWS, 512), f32),
            pltpu.VMEM((2, 4, SUBS, SUB_ROWS, 512), f32),
            pltpu.VMEM((4, PAIR_ROWS, 128), f32),
            pltpu.VMEM((8, PAIR_ROWS, 128), f32),
            pltpu.VMEM((32, 32, 128), f32),
            pltpu.VMEM((4, 128), f32),
            pltpu.VMEM((4, 4, 128), f32),
            pltpu.VMEM((8, 4, 128), f32),
            pltpu.VMEM((16, 2, 128), f32),
            dma((3,)), dma((2,)), dma((2,)), dma((2, 4, SUBS)), dma((2, 4, SUBS)),
            dma((8,)), dma((8,)), dma((8,)), dma((8,)), dma((8,)), dma((8,)),
            dma((4,)), dma((4,)), dma((8,)), dma((8,)), dma((16,)), dma((16,)),
        ],
        compiler_params=pltpu.CompilerParams(
            collective_id=0, has_side_effects=True, vmem_limit_bytes=56 * 1024 * 1024
        ),
        name="direct_term",
    )(trials, valence_factor.reshape(512, 256), conduction_factor.reshape(2048, 512), energy)
    return (applied, residual, quotient[:, 0])


def solution(mesh):
    split = Mesh(
        mesh.devices.reshape(8, 2, 2, mesh.shape["trial"], mesh.shape["val"]),
        ("x", "zh", "core", "trial", "val"),
    )
    in_specs = (P(None, None, "trial"), P(BLK, "val", None), P(BLK, "trial", None), P("val"), P("trial"))
    out_specs = (P(None, "val", "trial"), P(None, "val", "trial"), P())
    return jax.shard_map(on_device, mesh=split, in_specs=in_specs, out_specs=out_specs, check_vma=False)
```

time: 269 us -> 72.2 us (0.27)
  waiting for transfers between devices: 111 us -> 0 us
  blocking collectives: 107 us -> 0 us
  Pallas kernels: 0 us -> 64.7 us
  starting transfers between devices: 19.9 us -> 0 us
  between operations: 14.1 us -> 0.64 us
  matrix products: 6.46 us -> 0 us
    all_gather x1 -> x0, waiting for transfers between devices: 92.7 us -> none  [side_by_side(): lax.all_gather(both, axis, axis=dim, tiled=True)]
    pallas_call x0 -> x1, Pallas kernels: none -> 64.7 us  [on_device(): pl.pallas_call(kernel, out_shape=(jax.ShapeDtypeStruct((32, 32, 128), f32...]
    all_to_all x1 -> x0, blocking collectives: 56.1 us -> none  [sum_at_owner(): pieces = lax.all_to_all(split_up(shard, dim, peers), axis, 0, 0, tiled=True)]
    psum x5 -> x0, blocking collectives: 51.3 us -> none  [by_axis(): return functools.reduce(lax.psum, axes, shard)]
    all_to_all x1 -> x0, starting transfers between devices: 19.8 us -> none  [sum_at_owner(): pieces = lax.all_to_all(split_up(shard, dim, peers), axis, 0, 0, tiled=True)]
    all_to_all x1 -> x0, waiting for transfers between devices: 18.2 us -> none  [sum_at_owner(): pieces = lax.all_to_all(split_up(shard, dim, peers), axis, 0, 0, tiled=True)]
    dot_general x1 -> x0, matrix products: 6.46 us -> none  [on_device(): jnp.einsum('ptvc,pcd->tvd', inner, conduction_factor, preferred_element_t...]
    reduce_sum x5 -> x0, other arithmetic: 3.1 us -> none  [the longest x2 2.7 us: sum_at_owner(): return jnp.sum(pieces, axis=0)]
  transfers between devices with their start and end apart: 2 -> 0, of which waited for: 2 -> 0; matrix products, arithmetic and copies ran while one was open for 0% -> 0% of each run, Pallas kernels for 0% -> 0%
where the time goes in v1:
time: 72.2 us; the launch traced here: 71.8 us
  Pallas kernels  64.7 us (90%)
  local copies, waits for them, and re-layouts  5.08 us (7%)
  other arithmetic  1.35 us (2%)
    pallas_call x1, Pallas kernels, on_device(): pl.pallas_call(kernel, out_shape=(jax.ShapeDtypeStruct((32, 32, 128), f32...  64.7 us
    unnamed x2, local copies, waits for them, and re-layouts  3.73 us

profile of v1, /device:TPU:1, one launch (start us, length us, event | category | flops | bytes accessed | tf_op | source)
XLA Modules:
  0.0 71.8 jit_solution(9947517340138925930)
XLA Ops:
  0.6 1.3 %broadcast_subtract_fusion.energy_ref = f32[32,128]{1,0:T(8,128)} fusion(f32[32]{0:T(128)} %param.8, f32[128]{0:T(128)} %param.9), kind=kLoop, calls=%fused_computation.1 | loop fusion | flops 4096 | bytes 17024 | tf_op jit(solution)/shard_map/sub | solution.py:235
  2.0 64.7 %direct_term.1 = (f32[32,32,128]{2,1,0:T(8,128)}, f32[32,32,128]{2,1,0:T(8,128)}, f32[32,128]{1,0:T(8,128)}) custom-call(bf16[32,256,128]{2,1,0:T(8,128)(2,1)} %trials_hbm.1, bf16[512,256]{1,0:T(8,128)(2,1)} %bitcast.3, bf16[2048,512]{1,0:T(8,128)(2,1)} %bitcast.2, f32[32,128]{1,0:T(8,128)} %broadcast_subtract_fusion.energy_ref), custom_call_target="tpu_custom_call" | custom-call | tf_op jit(solution)/shard_map/direct_term/pallas_call | solution.py:240
  66.7 1.3 %slice_reduce_fusion = f32[32]{0:T(128)} fusion(f32[32,128]{1,0:T(8,128)} %get-tuple-element.8), kind=kLoop, calls=%fused_computation | loop fusion | bytes 256 | tf_op jit(solution)/shard_map/slice | solution.py:274
  68.1 1.9 %copy.10 = f32[32,32,128]{2,1,0:T(8,128)} copy(f32[32,32,128]{2,1,0:T(8,128)} %get-tuple-element.12) | data formatting | bytes 1048576
  69.9 1.9 %copy.11 = f32[32,32,128]{2,1,0:T(8,128)} copy(f32[32,32,128]{2,1,0:T(8,128)} %get-tuple-element.13) | data formatting | bytes 1048576

commit v2 on v1

--- a/solution.py
+++ b/solution.py
@@ -24,12 +24,12 @@
 
 
 def kernel(
-    trials_hbm, valence_hbm, conduction_hbm, energy_ref,
+    trials, valence, conduction, val_ref, cond_ref,
     applied_ref, residual_ref, quotient_ref,
-    trials, valence, conduction, left, outgoing, from_core, own, from_x, blocks, from_z,
-    gathered, sums, sums_z, sums_y, quotients,
-    load_sem, core_send, core_recv, x_send, x_recv, z_send, z_recv, g_send, g_recv,
-    f_send, f_recv, qz_send, qz_recv, qy_send, qy_recv, qx_send, qx_recv,
+    left, outgoing, from_core, own, from_x, blocks, from_z,
+    gathered, vectors, sums_y, sums_z, quotients,
+    core_send, core_recv, x_send, x_recv, z_send, z_recv, g_send, g_recv,
+    f_send, f_recv, t_send, t_recv, qy_send, qy_recv, qz_send, qz_recv, qx_send, qx_recv,
 ):
     x, zh, core = lax.axis_index("x"), lax.axis_index("zh"), lax.axis_index("core")
     zl, y = lax.axis_index("trial"), lax.axis_index("val")
@@ -52,21 +52,12 @@
             device_id=device, device_id_type=MESH,
         )
 
-    loads = [
-        pltpu.make_async_copy(valence_hbm, valence, load_sem.at[0]),
-        pltpu.make_async_copy(trials_hbm, trials, load_sem.at[1]),
-        pltpu.make_async_copy(conduction_hbm, conduction, load_sem.at[2]),
-    ]
-    for load in loads:
-        load.start()
     barrier = pltpu.get_barrier_semaphore()
     partners = [at_x(0, other)]
     for step in range(1, RING):
         partners += [at_x(step, core), at_x(step, other), at_z(step), at_y(step)]
     for device in partners:
         pl.semaphore_signal(barrier, inc=1, device_id=device, device_id_type=MESH)
-    loads[0].wait()
-    loads[1].wait()
 
     def unit(half, u):
         for q in range(4):
@@ -79,12 +70,16 @@
                     left[q * 64 + i * 32:q * 64 + i * 32 + 32, p * 128:(p + 1) * 128] = (
                         inner[p * 32:(p + 1) * 32, i * 128:(i + 1) * 128]
                     )
-        if half is other and u == 0:
-            loads[2].wait()
         return jnp.dot(left[...], conduction[...], preferred_element_type=jnp.float32)
 
+    mine = core * 16 + x * 2
+    v_rows = pl.ds(pl.multiple_of(y * 32, 32), 32)
+    for i in range(2):
+        vectors[0, i * 32:(i + 1) * 32] = trials[mine + i, v_rows, :].astype(jnp.float32)
+    small = []
     to_core = []
-    for u in range(2):
+
+    def exchange(u):
         outgoing[u] = unit(other, u)
         if u == 0:
             pl.semaphore_wait(barrier, len(partners))
@@ -107,6 +102,12 @@
         return (s < SUBS // 2) == (way == 0)
 
     for u in range(2):
+        exchange(u)
+        if u == 0:
+            for step, slot in ((1, 3), (7, 1), (2, 2)):
+                copy = remote(vectors.at[0], vectors.at[slot], t_send.at[slot], t_recv.at[slot], at_z(step))
+                copy.start()
+                small.append(copy)
         product = unit(core, u)
         to_core[u].wait_recv()
         for q in range(4):
@@ -142,29 +143,51 @@
         copy.start()
         z_copies[step] = copy
     from_z[0] = blocks[zl]
+
+    def slot_of(block):
+        return lax.rem(block + 4 - zl, 4)
+
+    seat_rows = lax.broadcasted_iota(jnp.int32, (32, 32), 0) == lax.broadcasted_iota(jnp.int32, (32, 32), 1)
+    val = jnp.sum(jnp.where(seat_rows, jnp.broadcast_to(val_ref[...], (32, 32)), 0.0), axis=1, keepdims=True)
+    energy = cond_ref[...] - val
+    for copy in small:
+        copy.wait_recv()
+    products, squares = [], []
+    for i in range(2):
+        rows = slice(i * 32, (i + 1) * 32)
+        product = vectors[slot_of(0), rows] * own[7, rows, 0:128]
+        for b in range(1, 4):
+            product = product + vectors[slot_of(b), rows] * own[7, rows, b * 128:(b + 1) * 128]
+        square = jnp.where(zh == 0, vectors[0, rows] * vectors[0, rows], 0.0)
+        product = product + energy * square
+        products.append(jnp.sum(product, axis=0, keepdims=True))
+        squares.append(jnp.sum(square, axis=0, keepdims=True))
+    sums_y[0] = jnp.concatenate(products + squares, axis=0)
+    y_copies = []
+    for step in (4, 3, 5, 2, 6, 1, 7):
+        copy = remote(sums_y.at[0], sums_y.at[step], qy_send.at[step], qy_recv.at[step], at_y(step))
+        copy.start()
+        y_copies.append(copy)
+    for copy in y_copies:
+        copy.wait_recv()
+    total = sums_y[ring(y + RING)]
+    for i in range(1, RING):
+        total = total + sums_y[ring(y + RING - i)]
+    sums_z[0] = total
+    q_copies = []
+    for step in (4, 3, 5, 2, 6, 1, 7):
+        copy = remote(sums_z.at[0], sums_z.at[step], qz_send.at[step], qz_recv.at[step], at_z(step))
+        copy.start()
+        q_copies.append(copy)
+
     for step in (1, 7, 2, 6, 3, 5, 4):
         z_copies[step].wait_recv()
     total = from_z[ring(z + RING)]
     for i in range(1, RING):
         total = total + from_z[ring(z + RING - i)]
-    mine = core * 16 + x * 2
-    v_rows = pl.ds(pl.multiple_of(y * 32, 32), 32)
-    energy = energy_ref[...]
-    products = []
-    squares = []
     for i in range(2):
-        vector = trials[mine + i, v_rows, :].astype(jnp.float32)
-        image = total[i * 32:(i + 1) * 32] + energy * vector
-        gathered[mine + i] = image
-        products.append(jnp.sum(vector * image, axis=0, keepdims=True))
-        squares.append(jnp.sum(vector * vector, axis=0, keepdims=True))
-    sums_z[0] = jnp.concatenate(products + squares, axis=0)
-
-    q_copies = []
-    for step, slot in ((1, 3), (7, 1), (2, 2)):
-        copy = remote(sums_z.at[0], sums_z.at[slot], qz_send.at[slot], qz_recv.at[slot], at_z(step))
-        copy.start()
-        q_copies.append(copy)
+        rows = slice(i * 32, (i + 1) * 32)
+        gathered[mine + i] = total[rows] + energy * vectors[0, rows]
     g_copies = {}
     pair = pl.ds(mine, 2)
     for step in (4, 3, 5, 2, 6, 1, 7):
@@ -183,58 +206,50 @@
         copy.start()
         f_copies[step] = copy
 
-    forward(0)
+    for step in (0, 1, 7):
+        forward(step)
     for copy in q_copies:
         copy.wait_recv()
-    total = sums_z[lax.rem(4 - zl, 4)]
-    for i in range(1, 4):
-        total = total + sums_z[lax.rem(4 - zl + i, 4)]
-    sums_y[0] = total
-    y_copies = []
-    for step in (4, 3, 5, 2, 6, 1, 7):
-        copy = remote(sums_y.at[0], sums_y.at[step], qy_send.at[step], qy_recv.at[step], at_y(step))
-        copy.start()
-        y_copies.append(copy)
-    for step in (1, 7, 2):
-        forward(step)
-    for copy in y_copies:
-        copy.wait_recv()
-    total = sums_y[ring(y + RING)]
+    total = sums_z[ring(z + RING)]
     for i in range(1, RING):
-        total = total + sums_y[ring(y + RING - i)]
+        total = total + sums_z[ring(z + RING - i)]
     lanes = jnp.sum(total, axis=1, keepdims=True)
     ratio = lanes[0:2] / (lanes[2:4] + 1e-6)
     seat = core * 8 + x
     quotients[seat] = jnp.broadcast_to(ratio, (2, 128))
-    for n in range(1, 16):
+    seat_copies = []
+    for n in range(2, 16):
         step, c = n // 2, (core if n % 2 == 0 else other)
         copy = remote(quotients.at[seat], quotients.at[seat], qx_send.at[n], qx_recv.at[n], at_x(step, c))
         copy.start()
-        q_copies.append(copy)
-    for step in (6, 3, 5, 4):
+        seat_copies.append(copy)
+    copy = remote(quotients.at[seat], quotients.at[seat], qx_send.at[1], qx_recv.at[1], at_x(0, other))
+    copy.start()
+    seat_copies.append(copy)
+    for step in (2, 6, 3, 5, 4):
         forward(step)
-    for copy in q_copies[3:]:
-        copy.wait_recv()
     for step in range(RING):
         f_copies[step].wait_recv()
+    applied_ref[...] = gathered[...]
+    for copy in seat_copies:
+        copy.wait_recv()
+    lane = lax.broadcasted_iota(jnp.int32, (1, 128), 1)
+    everyone = jnp.zeros((1, 128), jnp.float32)
     for n in range(16):
         for i in range(2):
             t = 2 * n + i
             row = quotients[n, i:i + 1, :]
-            image = gathered[t]
-            applied_ref[t] = image
-            residual_ref[t] = image - row * trials[t, v_rows, :].astype(jnp.float32)
-            quotient_ref[t:t + 1, :] = row
+            residual_ref[t] = gathered[t] - row * trials[t, v_rows, :].astype(jnp.float32)
+            everyone = jnp.where(lane == t, row, everyone)
+    quotient_ref[...] = everyone[:, 0:32]
     for group in (to_core, x_copies.values(), z_copies.values(), g_copies.values(), f_copies.values(),
-                  q_copies, y_copies):
+                  small, y_copies, q_copies, seat_copies):
         for copy in group:
             copy.wait_send()
 
 
 def on_device(trials, valence_factor, conduction_factor, val_energy, cond_energy):
-    energy = cond_energy[None, :] - val_energy[:, None]
     vmem = pl.BlockSpec(memory_space=pltpu.VMEM)
-    hbm = pl.BlockSpec(memory_space=pl.ANY)
     dma = pltpu.SemaphoreType.DMA
     f32 = jnp.float32
     applied, residual, quotient = pl.pallas_call(
@@ -242,14 +257,11 @@
         out_shape=(
             jax.ShapeDtypeStruct((32, 32, 128), f32),
             jax.ShapeDtypeStruct((32, 32, 128), f32),
-            jax.ShapeDtypeStruct((32, 128), f32),
+            jax.ShapeDtypeStruct((1, 32), f32),
         ),
-        in_specs=[hbm, hbm, hbm, vmem],
+        in_specs=[vmem] * 5,
         out_specs=(vmem, vmem, vmem),
         scratch_shapes=[
-            pltpu.VMEM((32, 256, 128), jnp.bfloat16),
-            pltpu.VMEM((512, 256), jnp.bfloat16),
-            pltpu.VMEM((2048, 512), jnp.bfloat16),
             pltpu.VMEM((256, 2048), jnp.bfloat16),
             pltpu.VMEM((2, 256, 512), f32),
             pltpu.VMEM((2, 256, 512), f32),
@@ -258,20 +270,21 @@
             pltpu.VMEM((4, PAIR_ROWS, 128), f32),
             pltpu.VMEM((8, PAIR_ROWS, 128), f32),
             pltpu.VMEM((32, 32, 128), f32),
-            pltpu.VMEM((4, 128), f32),
-            pltpu.VMEM((4, 4, 128), f32),
+            pltpu.VMEM((4, PAIR_ROWS, 128), f32),
+            pltpu.VMEM((8, 4, 128), f32),
             pltpu.VMEM((8, 4, 128), f32),
             pltpu.VMEM((16, 2, 128), f32),
-            dma((3,)), dma((2,)), dma((2,)), dma((2, 4, SUBS)), dma((2, 4, SUBS)),
+            dma((2,)), dma((2,)), dma((2, 4, SUBS)), dma((2, 4, SUBS)),
             dma((8,)), dma((8,)), dma((8,)), dma((8,)), dma((8,)), dma((8,)),
-            dma((4,)), dma((4,)), dma((8,)), dma((8,)), dma((16,)), dma((16,)),
+            dma((4,)), dma((4,)), dma((8,)), dma((8,)), dma((8,)), dma((8,)), dma((16,)), dma((16,)),
         ],
         compiler_params=pltpu.CompilerParams(
-            collective_id=0, has_side_effects=True, vmem_limit_bytes=56 * 1024 * 1024
+            collective_id=0, has_side_effects=True, vmem_limit_bytes=32 * 1024 * 1024
         ),
         name="direct_term",
-    )(trials, valence_factor.reshape(512, 256), conduction_factor.reshape(2048, 512), energy)
-    return (applied, residual, quotient[:, 0])
+    )(trials, valence_factor.reshape(512, 256), conduction_factor.reshape(2048, 512),
+      val_energy.reshape(1, 32), cond_energy.reshape(1, 128))
+    return (applied, residual, quotient.reshape(32))
 
 
 def solution(mesh):

time: 72.2 us -> 69.2 us (0.958)
  Pallas kernels: 64.7 us -> 60.7 us
  local copies, waits for them, and re-layouts: 5.08 us -> 7.53 us
  other arithmetic: 1.35 us -> 0 us
    pallas_call x1, Pallas kernels: 64.7 us -> 60.7 us  [on_device(): pl.pallas_call(kernel, out_shape=(jax.ShapeDtypeStruct((32, 32, 128), f32...]
    unnamed x2 -> x13, local copies, waits for them, and re-layouts: 3.73 us -> 7.53 us
    sub x1 -> x0, other arithmetic: 1.35 us -> none  [on_device(): energy = cond_energy[None, :] - val_energy[:, None]]
    slice x1 -> x0, local copies, waits for them, and re-layouts: 1.34 us -> none  [on_device(): return (applied, residual, quotient[:, 0])]
where the time goes in v2:
time: 69.2 us; the launch traced here: 68.9 us
  Pallas kernels  60.7 us (88%)
  local copies, waits for them, and re-layouts  7.53 us (11%)
    pallas_call x1, Pallas kernels, on_device(): pl.pallas_call(kernel, out_shape=(jax.ShapeDtypeStruct((32, 32, 128), f32...  60.7 us
    unnamed x13, local copies, waits for them, and re-layouts  7.53 us

profile of v2, /device:TPU:1, one launch (start us, length us, event | category | flops | bytes accessed | tf_op | source)
XLA Modules:
  0.0 68.9 jit_solution(6556314711923153292)
XLA Ops:
  0.6 0.0 copy-start
  0.6 1.6 %copy-done = bf16[32,256,128]{2,1,0:T(8,128)(2,1)S(1)} copy-done((bf16[32,256,128]{2,1,0:T(8,128)(2,1)S(1)}, bf16[32,256,128]{2,1,0:T(8,128)(2,1)}, u32[]{:S(2)}) %copy-start) | copy-done | bytes 2097176
  2.2 0.0 copy-start.1
  2.2 1.6 %copy-done.1 = bf16[16,128,512]{2,1,0:T(8,128)(2,1)S(1)} copy-done((bf16[16,128,512]{2,1,0:T(8,128)(2,1)S(1)}, bf16[16,128,512]{2,1,0:T(8,128)(2,1)}, u32[]{:S(2)}) %copy-start.1) | copy-done | bytes 2097176
  3.8 0.0 copy-start.2
  3.8 0.9 %copy-done.2 = bf16[16,32,256]{2,1,0:T(8,128)(2,1)S(1)} copy-done((bf16[16,32,256]{2,1,0:T(8,128)(2,1)S(1)}, bf16[16,32,256]{2,1,0:T(8,128)(2,1)}, u32[]{:S(2)}) %copy-start.2) | copy-done | bytes 262168
  4.8 0.0 copy-start.3
  4.8 0.7 copy-done.3
  5.4 0.0 copy-start.4
  5.4 0.7 copy-done.4
  6.1 60.7 %direct_term.1 = (f32[32,32,128]{2,1,0:T(8,128)S(1)}, f32[32,32,128]{2,1,0:T(8,128)S(1)}, f32[1,32]{1,0:T(1,128)S(1)}) custom-call(bf16[32,256,128]{2,1,0:T(8,128)(2,1)S(1)} %copy-done, bf16[512,256]{1,0:T(8,128)(2,1)S(1)} %bitcast.6, bf16[2048,512]{1,0:T(8,128)(2,1)S(1)} %bitcast.5, f32[1,32]{1,0:T(1,128)S(1)} %bitcast.7, f32[1,128]{1,0:T(1,128)S(1)} %bitcast.8), custom_call_target="tpu_custom_call" | custom-call | tf_op jit(solution)/shard_map/direct_term/pallas_call | solution.py:255
  66.8 0.8 %copy.11 = f32[32,32,128]{2,1,0:T(8,128)} copy(f32[32,32,128]{2,1,0:T(8,128)S(1)} %get-tuple-element.12) | data formatting | bytes 1048576
  67.6 0.8 %copy.12 = f32[32,32,128]{2,1,0:T(8,128)} copy(f32[32,32,128]{2,1,0:T(8,128)S(1)} %get-tuple-element.13) | data formatting | bytes 1048576
  68.4 0.5 copy.13
Async XLA Ops:
  0.6 1.6 %copy-start = (bf16[32,256,128]{2,1,0:T(8,128)(2,1)S(1)}, bf16[32,256,128]{2,1,0:T(8,128)(2,1)}, u32[]{:S(2)}) copy-start(bf16[32,256,128]{2,1,0:T(8,128)(2,1)} %trials.1) | copy-start | bytes 6291460
  2.2 1.6 %copy-start.1 = (bf16[16,128,512]{2,1,0:T(8,128)(2,1)S(1)}, bf16[16,128,512]{2,1,0:T(8,128)(2,1)}, u32[]{:S(2)}) copy-start(bf16[16,128,512]{2,1,0:T(8,128)(2,1)} %param.7) | copy-start | bytes 6291460
  3.8 0.9 %copy-start.2 = (bf16[16,32,256]{2,1,0:T(8,128)(2,1)S(1)}, bf16[16,32,256]{2,1,0:T(8,128)(2,1)}, u32[]{:S(2)}) copy-start(bf16[16,32,256]{2,1,0:T(8,128)(2,1)} %param.6) | copy-start | bytes 786436
  4.8 0.7 copy-start.3
  5.4 0.7 copy-start.4

commit v3 on v2

v3 whole, which is shorter than its diff:
```python
import jax
import jax.numpy as jnp
from jax import lax
from jax.experimental import pallas as pl
from jax.experimental.pallas import tpu as pltpu
from jax.sharding import Mesh
from jax.sharding import PartitionSpec as P

BLK = ("x", "zh", "core")
MESH = pl.DeviceIdType.MESH
RING = 8
PAIR_ROWS = 64
TARGET = (4, 3, 5, 2, 6, 1, 7, 0)
FAR_FIRST = (4, 3, 5, 2, 6, 1, 7)


def ring(i):
    return lax.rem(i, RING)


def kernel(
    trials_hbm, valence_hbm, conduction_hbm, val_hbm, cond_hbm,
    applied_ref, residual_ref, quotient_ref,
    trials, valence, conduction, val_ref, cond_ref, left, outgoing, from_core, own,
    from_4, from_3, from_2, from_1, blocks, from_z, vectors,
    below, above, beyond, part, from_x, half, other_half, whole,
    gathered, sums_y, sums_z, sums_x,
    load_sem, core_send, core_recv, a_send, a_recv, z_send, z_recv, t_send, t_recv,
    b_send, b_recv, x_send, x_recv, h_send, h_recv, g_send, g_recv, f_send, f_recv,
    qy_send, qy_recv, qz_send, qz_recv, qx_send, qx_recv,
):
    x, zh, core = lax.axis_index("x"), lax.axis_index("zh"), lax.axis_index("core")
    zl, y = lax.axis_index("trial"), lax.axis_index("val")
    z = zh * 4 + zl
    other = 1 - core

    def at_x(step, c):
        return {"x": ring(x + step), "zh": zh, "core": c, "trial": zl, "val": y}

    def at_z(step):
        there = ring(z + step)
        return {"x": x, "zh": there // 4, "core": core, "trial": lax.rem(there, 4), "val": y}

    def at_y(step):
        return {"x": x, "zh": zh, "core": core, "trial": zl, "val": ring(y + step)}

    def remote(src, dst, send, recv, device):
        return pltpu.make_async_remote_copy(
            src_ref=src, dst_ref=dst, send_sem=send, recv_sem=recv,
            device_id=device, device_id_type=MESH,
        )

    loads = [
        pltpu.make_async_copy(src, dst, load_sem.at[i])
        for i, (src, dst) in enumerate((
            (valence_hbm, valence), (trials_hbm, trials), (conduction_hbm, conduction),
            (val_hbm, val_ref), (cond_hbm, cond_ref),
        ))
    ]
    for load in loads:
        load.start()
    barrier = pltpu.get_barrier_semaphore()
    partners = [at_x(0, other)]
    for step in range(1, RING):
        partners += [at_x(step, core), at_x(step, other), at_z(step), at_y(step)]
    for device in partners:
        pl.semaphore_signal(barrier, inc=1, device_id=device, device_id_type=MESH)
    loads[0].wait()
    loads[1].wait()

    def unit(side, u):
        for q in range(4):
            first = 16 * side + 2 * ring(x + TARGET[4 * u + q])
            pair = jnp.concatenate([trials[first], trials[first + 1]], axis=1)
            inner = jnp.dot(valence[...], pair, preferred_element_type=jnp.float32)
            inner = inner.astype(jnp.bfloat16)
            for p in range(16):
                for i in range(2):
                    left[q * 64 + i * 32:q * 64 + i * 32 + 32, p * 128:(p + 1) * 128] = (
                        inner[p * 32:(p + 1) * 32, i * 128:(i + 1) * 128]
                    )
        if side is other and u == 0:
            loads[2].wait()
        return jnp.dot(left[...], conduction[...], preferred_element_type=jnp.float32)

    mine = core * 16 + x * 2
    v_rows = pl.ds(pl.multiple_of(y * 32, 32), 32)
    for i in range(2):
        vectors[0, i * 32:(i + 1) * 32] = trials[mine + i, v_rows, :].astype(jnp.float32)

    def trial_copies():
        return [
            remote(vectors.at[0], vectors.at[slot], t_send.at[slot], t_recv.at[slot], at_z(step))
            for step, slot in ((1, 3), (7, 1), (2, 2))
        ]

    def along_x(kind, way):
        n = kind * 2 + way
        send, recv = a_send.at[n], a_recv.at[n]
        if kind == 0:
            src, dst = own.at[0, pl.ds(32 * way, 32)], from_4.at[way]
        else:
            slot = ((1, 2), (3, 4), (5, 6))[kind - 1][way]
            src, dst = own.at[slot], (from_3, from_2, from_1)[kind - 1].at[way]
        reach = (2, 1, 2, 1)[kind]
        return remote(src, dst, send, recv, at_x((reach, RING - reach)[way], core))

    def block_of(step, u):
        column = pl.multiple_of(lax.rem(zl + step, 4) * 128, 128)
        return own.at[pl.ds(4 * u, 4), pl.ds(0, PAIR_ROWS), pl.ds(column, 128)]

    def along_z(u):
        far = (2, 6)[u]
        return [
            remote(block_of(far, u), beyond.at[u], b_send.at[4 + u], b_recv.at[4 + u], at_z(far)),
            remote(block_of(1, u), below.at[u], b_send.at[u], b_recv.at[u], at_z(1)),
            remote(block_of(7, u), above.at[u], b_send.at[2 + u], b_recv.at[2 + u], at_z(7)),
        ]

    to_core = []
    for u in range(2):
        outgoing[u] = unit(other, u)
        if u == 0:
            pl.semaphore_wait(barrier, len(partners))
        copy = remote(outgoing.at[u], from_core.at[u], core_send.at[u], core_recv.at[u], at_x(0, other))
        copy.start()
        to_core.append(copy)
        if u == 0:
            @pl.when(core == 0)
            def _():
                for copy in trial_copies():
                    copy.start()
        product = unit(core, u)
        to_core[u].wait_recv()
        for q in range(4):
            own[4 * u + q] = product[q * 64:(q + 1) * 64] + from_core[u, q * 64:(q + 1) * 64]

        @pl.when(core == 0)
        def _():
            if u == 0:
                for kind in (0, 1):
                    for way in range(2):
                        along_x(kind, way).start()
            else:
                for way in range(2):
                    along_x(0, way).wait_recv()
                    along_x(1, way).wait_recv()
                    slot, rows = 3 + way, slice(32 * way, 32 * way + 32)
                    own[slot] = own[slot] + from_3[way]
                    own[slot, rows] = own[slot, rows] + from_4[way]
                    along_x(2, way).start()
                for way in range(2):
                    along_x(3, way).start()

        @pl.when(core == 1)
        def _():
            for copy in along_z(u):
                copy.start()

    loads[3].wait()
    loads[4].wait()
    on_diagonal = lax.broadcasted_iota(jnp.int32, (32, 128), 0) == lax.broadcasted_iota(jnp.int32, (32, 128), 1)
    val_row = jnp.concatenate([val_ref[...], jnp.zeros((1, 96), jnp.float32)], axis=1)
    energy = cond_ref[...] - jnp.sum(jnp.where(on_diagonal, val_row, 0.0), axis=1, keepdims=True)

    def in_lanes(values, first):
        count = values.shape[0]
        column = jnp.sum(values, axis=1, keepdims=True)
        lane = lax.broadcasted_iota(jnp.int32, (count, 128), 1)
        row = lax.broadcasted_iota(jnp.int32, (count, 128), 0)
        return jnp.sum(jnp.where(lane == row + first, column, 0.0), axis=0, keepdims=True)

    def over_rows(values):
        return jnp.sum(values, axis=0, keepdims=True)

    fixed, squares = [], []
    for i in range(2):
        vector = vectors[0, i * 32:(i + 1) * 32]
        square = jnp.where(zh == 0, vector * vector, 0.0)
        fixed.append(over_rows(energy * square))
        squares.append(over_rows(square))
    fixed = in_lanes(jnp.concatenate(fixed, axis=0), mine)
    sums_y[0, 1:2] = in_lanes(jnp.concatenate(squares, axis=0), mine)

    def z_copy(step):
        return remote(blocks.at[lax.rem(zl + step, 4)], from_z.at[step], z_send.at[step], z_recv.at[step], at_z(step))

    def x_copy(step):
        return remote(part.at[ring(x + step)], from_x.at[step], x_send.at[step], x_recv.at[step], at_x(step, core))

    def half_copy():
        return remote(half, other_half, h_send.at[0], h_recv.at[0], at_z(4))

    @pl.when(core == 0)
    def _():
        for kind in (3, 2):
            for way in range(2):
                along_x(kind, way).wait_recv()
        summed = own[7] + from_1[0] + from_1[1] + from_2[0] + from_2[1]
        for b in range(4):
            blocks[b] = summed[:, b * 128:(b + 1) * 128]
        for step in FAR_FIRST:
            z_copy(step).start()
        from_z[0] = blocks[zl]
        for copy in trial_copies():
            copy.wait_recv()
        products = []
        for i in range(2):
            rows = slice(i * 32, (i + 1) * 32)
            product = vectors[0, rows] * blocks[zl, rows]
            for b in range(1, 4):
                product = product + vectors[b, rows] * blocks[lax.rem(zl + b, 4), rows]
            products.append(over_rows(product))
        sums_y[0, 0:1] = fixed + in_lanes(jnp.concatenate(products, axis=0), mine)

    @pl.when(core == 1)
    def _():
        products = [None] * 16
        column = pl.ds(pl.multiple_of(zl * 128, 128), 128)
        for u in range(2):
            for copy in along_z(u):
                copy.wait_recv()
            for q in range(4):
                k = 4 * u + q
                part[ring(x + TARGET[k])] = own[k, :, column] + below[u, q] + above[u, q] + beyond[u, q]
        for step in FAR_FIRST:
            x_copy(step).start()
        for t in range(16):
            image = part[t // 2, (t % 2) * 32:(t % 2) * 32 + 32]
            products[t] = over_rows(image * trials[16 + t, v_rows, :].astype(jnp.float32))
        sums_y[0, 0:1] = fixed + in_lanes(jnp.concatenate(products, axis=0), 16)

    y_copies = []
    for step in FAR_FIRST:
        copy = remote(sums_y.at[0], sums_y.at[step], qy_send.at[step], qy_recv.at[step], at_y(step))
        copy.start()
        y_copies.append(copy)
    for copy in y_copies:
        copy.wait_recv()
    total = sums_y[ring(y + RING)]
    for i in range(1, RING):
        total = total + sums_y[ring(y + RING - i)]
    sums_z[0] = total
    q_copies = []
    for step in FAR_FIRST:
        copy = remote(sums_z.at[0], sums_z.at[step], qz_send.at[step], qz_recv.at[step], at_z(step))
        copy.start()
        q_copies.append(copy)

    @pl.when(core == 0)
    def _():
        for step in reversed(FAR_FIRST):
            z_copy(step).wait_recv()
        total = from_z[ring(z + RING)]
        for i in range(1, RING):
            total = total + from_z[ring(z + RING - i)]
        whole[...] = total

    @pl.when(core == 1)
    def _():
        total = part[x]
        for step in reversed(FAR_FIRST):
            x_copy(step).wait_recv()
            total = total + from_x[step]
        half[...] = total
        half_copy().start()
        half_copy().wait_recv()
        whole[...] = half[...] + other_half[...]

    for i in range(2):
        rows = slice(i * 32, (i + 1) * 32)
        gathered[mine + i] = whole[rows] + energy * vectors[0, rows]
    g_copies = {}
    pair = pl.ds(mine, 2)
    for step in FAR_FIRST:
        copy = remote(gathered.at[pair], gathered.at[pair], g_send.at[step], g_recv.at[step], at_x(step, core))
        copy.start()
        g_copies[step] = copy
    f_copies = {}

    def forward(step):
        there = pl.ds(core * 16 + 2 * ring(x + RING - step), 2)
        if step:
            g_copies[step].wait_recv()
        copy = remote(gathered.at[there], gathered.at[there], f_send.at[step], f_recv.at[step], at_x(0, other))
        copy.start()
        f_copies[step] = copy

    forward(0)
    for copy in q_copies:
        copy.wait_recv()
    total = sums_z[ring(z + RING)]
    for i in range(1, RING):
        total = total + sums_z[ring(z + RING - i)]
    seat = core * 8 + x
    sums_x[seat] = total
    seat_copies = []
    for n in list(range(2, 16)) + [1]:
        step, c = n // 2, (core if n % 2 == 0 else other)
        copy = remote(sums_x.at[seat], sums_x.at[seat], qx_send.at[n], qx_recv.at[n], at_x(step, c))
        copy.start()
        seat_copies.append(copy)
    for step in reversed(FAR_FIRST):
        forward(step)
    for copy in seat_copies:
        copy.wait_recv()
    total = sums_x[0]
    for n in range(1, 16):
        total = total + sums_x[n]
    ratio = total[0:1] / (total[1:2] + 1e-6)
    quotient_ref[...] = ratio[:, 0:32]
    quotients = jnp.sum(jnp.where(on_diagonal, ratio, 0.0), axis=1, keepdims=True)
    for step in range(RING):
        f_copies[step].wait_recv()
    for t in range(32):
        image = gathered[t]
        applied_ref[t] = image
        residual_ref[t] = image - quotients[t:t + 1, :] * trials[t, v_rows, :].astype(jnp.float32)

    @pl.when(core == 0)
    def _():
        for copy in trial_copies():
            copy.wait_send()
        for kind in range(4):
            for way in range(2):
                along_x(kind, way).wait_send()
        for step in FAR_FIRST:
            z_copy(step).wait_send()

    @pl.when(core == 1)
    def _():
        for u in range(2):
            for copy in along_z(u):
                copy.wait_send()
        for step in FAR_FIRST:
            x_copy(step).wait_send()
        half_copy().wait_send()

    for group in (to_core, g_copies.values(), f_copies.values(), y_copies, q_copies, seat_copies):
        for copy in group:
            copy.wait_send()


def on_device(trials, valence_factor, conduction_factor, val_energy, cond_energy):
    vmem = pl.BlockSpec(memory_space=pltpu.VMEM)
    hbm = pl.BlockSpec(memory_space=pltpu.HBM)
    dma = pltpu.SemaphoreType.DMA
    f32 = jnp.float32
    applied, residual, quotient = pl.pallas_call(
        kernel,
        out_shape=(
            jax.ShapeDtypeStruct((32, 32, 128), f32),
            jax.ShapeDtypeStruct((32, 32, 128), f32),
            jax.ShapeDtypeStruct((1, 32), f32),
        ),
        in_specs=[hbm] * 5,
        out_specs=(vmem, vmem, vmem),
        scratch_shapes=[
            pltpu.VMEM((32, 256, 128), jnp.bfloat16),
            pltpu.VMEM((512, 256), jnp.bfloat16),
            pltpu.VMEM((2048, 512), jnp.bfloat16),
            pltpu.VMEM((1, 32), f32),
            pltpu.VMEM((1, 128), f32),
            pltpu.VMEM((256, 2048), jnp.bfloat16),
            pltpu.VMEM((2, 256, 512), f32),
            pltpu.VMEM((2, 256, 512), f32),
            pltpu.VMEM((8, PAIR_ROWS, 512), f32),
            pltpu.VMEM((2, 32, 512), f32),
            pltpu.VMEM((2, PAIR_ROWS, 512), f32),
            pltpu.VMEM((2, PAIR_ROWS, 512), f32),
            pltpu.VMEM((2, PAIR_ROWS, 512), f32),
            pltpu.VMEM((4, PAIR_ROWS, 128), f32),
            pltpu.VMEM((8, PAIR_ROWS, 128), f32),
            pltpu.VMEM((4, PAIR_ROWS, 128), f32),
            pltpu.VMEM((2, 4, PAIR_ROWS, 128), f32),
            pltpu.VMEM((2, 4, PAIR_ROWS, 128), f32),
            pltpu.VMEM((2, 4, PAIR_ROWS, 128), f32),
            pltpu.VMEM((8, PAIR_ROWS, 128), f32),
            pltpu.VMEM((8, PAIR_ROWS, 128), f32),
            pltpu.VMEM((PAIR_ROWS, 128), f32),
            pltpu.VMEM((PAIR_ROWS, 128), f32),
            pltpu.VMEM((PAIR_ROWS, 128), f32),
            pltpu.VMEM((32, 32, 128), f32),
            pltpu.VMEM((8, 2, 128), f32),
            pltpu.VMEM((8, 2, 128), f32),
            pltpu.VMEM((16, 2, 128), f32),
            dma((5,)), dma((2,)), dma((2,)), dma((8,)), dma((8,)), dma((8,)), dma((8,)), dma((4,)), dma((4,)),
            dma((6,)), dma((6,)), dma((8,)), dma((8,)), dma((1,)), dma((1,)), dma((8,)), dma((8,)),
            dma((8,)), dma((8,)), dma((8,)), dma((8,)), dma((8,)), dma((8,)), dma((16,)), dma((16,)),
        ],
        compiler_params=pltpu.CompilerParams(
            collective_id=0, has_side_effects=True, vmem_limit_bytes=32 * 1024 * 1024
        ),
        name="direct_term",
    )(*(pltpu.with_memory_space_constraint(a, pltpu.HBM) for a in (
        trials, valence_factor.reshape(512, 256), conduction_factor.reshape(2048, 512),
        val_energy.reshape(1, 32), cond_energy.reshape(1, 128),
    )))
    return (applied, residual, quotient.reshape(32))


def solution(mesh):
    split = Mesh(
        mesh.devices.reshape(8, 2, 2, mesh.shape["trial"], mesh.shape["val"]),
        ("x", "zh", "core", "trial", "val"),
    )
    in_specs = (P(None, None, "trial"), P(BLK, "val", None), P(BLK, "trial", None), P("val"), P("trial"))
    out_specs = (P(None, "val", "trial"), P(None, "val", "trial"), P())
    return jax.shard_map(on_device, mesh=split, in_specs=in_specs, out_specs=out_specs, check_vma=False)
```

time: 69.2 us -> 58.3 us (0.84)
  local copies, waits for them, and re-layouts: 7.53 us -> 2.1 us
  Pallas kernels: 60.7 us -> 55.4 us
    unnamed x13 -> x3, local copies, waits for them, and re-layouts: 7.53 us -> 2.1 us
    pallas_call x1, Pallas kernels: 60.7 us -> 55.4 us  [on_device(): pl.pallas_call(kernel, out_shape=(jax.ShapeDtypeStruct((32, 32, 128), f32...]
where the time goes in v3:
time: 58.3 us; the launch traced here: 58.1 us
  Pallas kernels  55.4 us (95%)
  local copies, waits for them, and re-layouts  2.1 us (4%)
  between operations  0.64 us (1%)
    pallas_call x1, Pallas kernels, on_device(): pl.pallas_call(kernel, out_shape=(jax.ShapeDtypeStruct((32, 32, 128), f32...  55.4 us
    unnamed x3, local copies, waits for them, and re-layouts  2.1 us

profile of v3, /device:TPU:1, one launch (start us, length us, event | category | flops | bytes accessed | tf_op | source)
XLA Modules:
  0.0 58.1 jit_solution(14343510113549102628)
XLA Ops:
  0.6 55.4 %direct_term.1 = (f32[32,32,128]{2,1,0:T(8,128)S(1)}, f32[32,32,128]{2,1,0:T(8,128)S(1)}, f32[1,32]{1,0:T(1,128)S(1)}) custom-call(bf16[32,256,128]{2,1,0:T(8,128)(2,1)} %trials_hbm.1, bf16[512,256]{1,0:T(8,128)(2,1)} %bitcast.7, bf16[2048,512]{1,0:T(8,128)(2,1)} %bitcast.6, f32[1,32]{1,0:T(1,128)} %bitcast.8, f32[1,128]{1,0:T(1,128)} %bitcast.9), custom_call_target="tpu_custom_call" | custom-call | tf_op jit(solution)/shard_map/direct_term/pallas_call | solution.py:349
  56.0 0.8 %copy.11 = f32[32,32,128]{2,1,0:T(8,128)} copy(f32[32,32,128]{2,1,0:T(8,128)S(1)} %get-tuple-element.12) | data formatting | bytes 1048576
  56.8 0.8 %copy.12 = f32[32,32,128]{2,1,0:T(8,128)} copy(f32[32,32,128]{2,1,0:T(8,128)S(1)} %get-tuple-element.13) | data formatting | bytes 1048576
  57.6 0.5 copy.13

commit v4 on v3

--- a/solution.py
+++ b/solution.py
@@ -94,16 +94,15 @@
             for step, slot in ((1, 3), (7, 1), (2, 2))
         ]
 
-    def along_x(kind, way):
-        n = kind * 2 + way
-        send, recv = a_send.at[n], a_recv.at[n]
-        if kind == 0:
-            src, dst = own.at[0, pl.ds(32 * way, 32)], from_4.at[way]
-        else:
-            slot = ((1, 2), (3, 4), (5, 6))[kind - 1][way]
-            src, dst = own.at[slot], (from_3, from_2, from_1)[kind - 1].at[way]
+    def along_x(kind, way, s):
+        n = (kind * 2 + way) * 2 + s
+        slot = ((0, 0), (1, 2), (3, 4), (5, 6))[kind][way]
+        rows = pl.ds(32 * s, 32)
+        dst = (from_4, from_3, from_2, from_1)[kind].at[way, rows]
         reach = (2, 1, 2, 1)[kind]
-        return remote(src, dst, send, recv, at_x((reach, RING - reach)[way], core))
+        return remote(own.at[slot, rows], dst, a_send.at[n], a_recv.at[n], at_x((reach, RING - reach)[way], core))
+
+    along_x_all = [(kind, way, s) for kind in range(4) for way in range(2) for s in range(2) if kind or s == way]
 
     def block_of(step, u):
         column = pl.multiple_of(lax.rem(zl + step, 4) * 128, 128)
@@ -138,19 +137,27 @@
         @pl.when(core == 0)
         def _():
             if u == 0:
-                for kind in (0, 1):
-                    for way in range(2):
-                        along_x(kind, way).start()
+                for way in range(2):
+                    along_x(0, way, way).start()
+                for way in range(2):
+                    along_x(1, way, 1 - way).start()
+                for way in range(2):
+                    along_x(1, way, way).start()
             else:
                 for way in range(2):
-                    along_x(0, way).wait_recv()
-                    along_x(1, way).wait_recv()
-                    slot, rows = 3 + way, slice(32 * way, 32 * way + 32)
-                    own[slot] = own[slot] + from_3[way]
-                    own[slot, rows] = own[slot, rows] + from_4[way]
-                    along_x(2, way).start()
-                for way in range(2):
-                    along_x(3, way).start()
+                    for s in range(2):
+                        along_x(3, way, s).start()
+                for way in range(2):
+                    s, slot, rows = 1 - way, 3 + way, slice(32 - 32 * way, 64 - 32 * way)
+                    along_x(1, way, s).wait_recv()
+                    own[slot, rows] = own[slot, rows] + from_3[way, rows]
+                    along_x(2, way, s).start()
+                for way in range(2):
+                    s, slot, rows = way, 3 + way, slice(32 * way, 32 * way + 32)
+                    along_x(1, way, s).wait_recv()
+                    along_x(0, way, s).wait_recv()
+                    own[slot, rows] = own[slot, rows] + from_3[way, rows] + from_4[way, rows]
+                    along_x(2, way, s).start()
 
         @pl.when(core == 1)
         def _():
@@ -195,7 +202,8 @@
     def _():
         for kind in (3, 2):
             for way in range(2):
-                along_x(kind, way).wait_recv()
+                for s in range(2):
+                    along_x(kind, way, s).wait_recv()
         summed = own[7] + from_1[0] + from_1[1] + from_2[0] + from_2[1]
         for b in range(4):
             blocks[b] = summed[:, b * 128:(b + 1) * 128]
@@ -223,8 +231,8 @@
             for q in range(4):
                 k = 4 * u + q
                 part[ring(x + TARGET[k])] = own[k, :, column] + below[u, q] + above[u, q] + beyond[u, q]
-        for step in FAR_FIRST:
-            x_copy(step).start()
+                if TARGET[k]:
+                    x_copy(TARGET[k]).start()
         for t in range(16):
             image = part[t // 2, (t % 2) * 32:(t % 2) * 32 + 32]
             products[t] = over_rows(image * trials[16 + t, v_rows, :].astype(jnp.float32))
@@ -235,6 +243,16 @@
         copy = remote(sums_y.at[0], sums_y.at[step], qy_send.at[step], qy_recv.at[step], at_y(step))
         copy.start()
         y_copies.append(copy)
+
+    @pl.when(core == 1)
+    def _():
+        total = part[x]
+        for step in FAR_FIRST:
+            x_copy(step).wait_recv()
+            total = total + from_x[step]
+        half[...] = total
+        half_copy().start()
+
     for copy in y_copies:
         copy.wait_recv()
     total = sums_y[ring(y + RING)]
@@ -258,12 +276,6 @@
 
     @pl.when(core == 1)
     def _():
-        total = part[x]
-        for step in reversed(FAR_FIRST):
-            x_copy(step).wait_recv()
-            total = total + from_x[step]
-        half[...] = total
-        half_copy().start()
         half_copy().wait_recv()
         whole[...] = half[...] + other_half[...]
 
@@ -321,9 +333,8 @@
     def _():
         for copy in trial_copies():
             copy.wait_send()
-        for kind in range(4):
-            for way in range(2):
-                along_x(kind, way).wait_send()
+        for kind, way, s in along_x_all:
+            along_x(kind, way, s).wait_send()
         for step in FAR_FIRST:
             z_copy(step).wait_send()
 
@@ -339,6 +350,19 @@
     for group in (to_core, g_copies.values(), f_copies.values(), y_copies, q_copies, seat_copies):
         for copy in group:
             copy.wait_send()
+
+
+def write_out(applied, residual, quotient, applied_hbm, residual_hbm, quotient_hbm, sems):
+    copies = [
+        pltpu.make_async_copy(src, dst, sems.at[i])
+        for i, (src, dst) in enumerate((
+            (applied, applied_hbm), (residual, residual_hbm), (quotient, quotient_hbm),
+        ))
+    ]
+    for copy in copies:
+        copy.start()
+    for copy in copies:
+        copy.wait()
 
 
 def on_device(trials, valence_factor, conduction_factor, val_energy, cond_energy):
@@ -365,7 +389,7 @@
             pltpu.VMEM((2, 256, 512), f32),
             pltpu.VMEM((2, 256, 512), f32),
             pltpu.VMEM((8, PAIR_ROWS, 512), f32),
-            pltpu.VMEM((2, 32, 512), f32),
+            pltpu.VMEM((2, PAIR_ROWS, 512), f32),
             pltpu.VMEM((2, PAIR_ROWS, 512), f32),
             pltpu.VMEM((2, PAIR_ROWS, 512), f32),
             pltpu.VMEM((2, PAIR_ROWS, 512), f32),
@@ -384,7 +408,7 @@
             pltpu.VMEM((8, 2, 128), f32),
             pltpu.VMEM((8, 2, 128), f32),
             pltpu.VMEM((16, 2, 128), f32),
-            dma((5,)), dma((2,)), dma((2,)), dma((8,)), dma((8,)), dma((8,)), dma((8,)), dma((4,)), dma((4,)),
+            dma((5,)), dma((2,)), dma((2,)), dma((16,)), dma((16,)), dma((8,)), dma((8,)), dma((4,)), dma((4,)),
             dma((6,)), dma((6,)), dma((8,)), dma((8,)), dma((1,)), dma((1,)), dma((8,)), dma((8,)),
             dma((8,)), dma((8,)), dma((8,)), dma((8,)), dma((8,)), dma((8,)), dma((16,)), dma((16,)),
         ],
@@ -396,6 +420,19 @@
         trials, valence_factor.reshape(512, 256), conduction_factor.reshape(2048, 512),
         val_energy.reshape(1, 32), cond_energy.reshape(1, 128),
     )))
+    applied, residual, quotient = pl.pallas_call(
+        write_out,
+        out_shape=(
+            jax.ShapeDtypeStruct((32, 32, 128), f32),
+            jax.ShapeDtypeStruct((32, 32, 128), f32),
+            jax.ShapeDtypeStruct((1, 32), f32),
+        ),
+        in_specs=[vmem] * 3,
+        out_specs=(hbm, hbm, hbm),
+        scratch_shapes=[dma((3,))],
+        compiler_params=pltpu.CompilerParams(vmem_limit_bytes=1024 * 1024),
+        name="write_out",
+    )(applied, residual, quotient)
     return (applied, residual, quotient.reshape(32))
 
 

time: 58.3 us -> 55.4 us (0.950)
  local copies, waits for them, and re-layouts: 2.1 us -> 0 us
  Pallas kernels: 55.4 us -> 54.7 us
    unnamed x3 -> x0, local copies, waits for them, and re-layouts: 2.1 us -> none
    pallas_call x1, Pallas kernels: 55.4 us -> 53.7 us  [on_device(): pl.pallas_call(kernel, out_shape=(jax.ShapeDtypeStruct((32, 32, 128), f32...]
    pallas_call x0 -> x1, Pallas kernels: none -> 1 us  [on_device(): pl.pallas_call(write_out, out_shape=(jax.ShapeDtypeStruct((32, 32, 128),...]
where the time goes in v4:
time: 55.4 us; the launch traced here: 55.3 us
  Pallas kernels  54.7 us (99%)
  between operations  0.64 us (1%)
    pallas_call x1, Pallas kernels, on_device(): pl.pallas_call(kernel, out_shape=(jax.ShapeDtypeStruct((32, 32, 128), f32...  53.7 us

profile of v4, /device:TPU:1, one launch (start us, length us, event | category | flops | bytes accessed | tf_op | source)
XLA Modules:
  0.0 55.3 jit_solution(10491106397152787306)
XLA Ops:
  0.6 53.7 %direct_term.1 = (f32[32,32,128]{2,1,0:T(8,128)S(1)}, f32[32,32,128]{2,1,0:T(8,128)S(1)}, f32[1,32]{1,0:T(1,128)S(1)}) custom-call(bf16[32,256,128]{2,1,0:T(8,128)(2,1)} %trials_hbm.1, bf16[512,256]{1,0:T(8,128)(2,1)} %bitcast.6, bf16[2048,512]{1,0:T(8,128)(2,1)} %bitcast.5, f32[1,32]{1,0:T(1,128)} %bitcast.7, f32[1,128]{1,0:T(1,128)} %bitcast.8), custom_call_target="tpu_custom_call" | custom-call | tf_op jit(solution)/shard_map/direct_term/pallas_call | solution.py:373
  54.3 1.0 %write_out.1 = (f32[32,32,128]{2,1,0:T(8,128)}, f32[32,32,128]{2,1,0:T(8,128)}, f32[1,32]{1,0:T(1,128)}) custom-call(f32[32,32,128]{2,1,0:T(8,128)S(1)} %get-tuple-element.9.applied, f32[32,32,128]{2,1,0:T(8,128)S(1)} %get-tuple-element.10.residual, f32[1,32]{1,0:T(1,128)S(1)} %get-tuple-element.11.quotient), custom_call_target="tpu_custom_call" | custom-call | tf_op jit(solution)/shard_map/write_out/pallas_call | solution.py:423
